TPU v7x, 256 devices: a whole 4x4x8 slice. The times are simulated.
256 devices in a mesh: dp: 32 (over z, y), tensor: 8 (over x, core).
Axes of the slice: x: 4, y: 4, z: 8, core: 2. Of those that a mesh axis runs over, the one named last changes fastest.
Arguments:
- hidden: bfloat16 [4096, 26624], P('dp', 'tensor'), may hold values from -6 to 6
- out_grad: bfloat16 [4096, 8192], P(('dp', 'tensor')), may hold values from -0.375 to 0.375
- master: float32 [8192, 26624], P('dp', 'tensor'), may hold values from -0.3125 to 0.3125
- first_moment: bfloat16 [8192, 26624], P('dp', 'tensor'), may hold values from -4 to 4
- second_moment: bfloat16 [8192, 26624], P('dp', 'tensor'), may hold values from 0.049804688 to 1
- row_counts: int32 [8], replicated, may hold values from 2816 to 3840, as said below
- step_count: int32 [1], replicated, may hold values from 1 to 11
Outputs:
- adam_update: float32 [8192, 26624], P('dp', 'tensor')
- weights_tp: bfloat16 [8192, 30720], P('dp', 'tensor')
Inputs may be any that keep to these rules, and one draw needn't show every extreme that they name: Tensor index j takes row_counts[j] consecutive hidden units in order; they sum to 26624; offsets[j] differs from j * 3328 by at most 256; the largest count equals 3840.
All inputs are finite; a program needn't handle non-finite values.
Results may differ from a plain program's by a relative error of at most 0.0045.
Values may be sent and summed in bfloat16 or wider, within the bound.
No kernel may reach another device: no remote copies, remote signals or barrier semaphores. Data moves between devices by JAX's collectives and lax.ppermute only.
A program may use at most 192 MiB of HBM per device.

v0:
```python
import jax
import jax.numpy as jnp
import numpy as np
from jax import lax
from jax.sharding import Mesh, PartitionSpec as P

DRIFT = 256
CAP = 3840
CHUNKS = ((0, 896), (2432, 3328), (896, 1664), (1664, 2432))
beta_first = 0.9
beta_second = 0.95
epsilon = 1e-08
decay_rate = 0.1
learn_rate = 0.001
TENSOR = ("x", "core")


def adamw(gradient, master, first_moment, second_moment, first_fix, second_fix):
    first_new = beta_first * first_moment + (1.0 - beta_first) * gradient
    second_new = beta_second * second_moment + (1.0 - beta_second) * gradient * gradient
    update = (
        first_new / first_fix / (jnp.sqrt(second_new / second_fix) + epsilon) + decay_rate * master
    )
    master_new = master - learn_rate * update
    return (master_new, update)


def per_device(hidden, out_grad, master, first_moment, second_moment, row_counts, step_count):
    width = hidden.shape[1]
    tensor_count = lax.axis_size(TENSOR)
    z_count = lax.axis_size("z")
    local_tokens = out_grad.shape[0]
    features = out_grad.shape[1] // z_count
    regrouped = lax.all_to_all(out_grad, "z", split_axis=1, concat_axis=0, tiled=True)
    spread = lax.all_gather(regrouped, TENSOR, axis=0, tiled=True)
    cotangent = spread.reshape(tensor_count, z_count, local_tokens, features)
    cotangent = cotangent.transpose(1, 0, 2, 3).reshape(-1, features)
    steps_done = step_count[0].astype(jnp.float32)
    first_fix = 1.0 - jnp.power(beta_first, steps_done)
    second_fix = 1.0 - jnp.power(beta_second, steps_done)
    gathered = [
        lax.all_gather(hidden[:, low:high], "z", axis=0, tiled=True) for low, high in CHUNKS
    ]
    updates = {}
    weights = {}
    for (low, high), acts in zip(CHUNKS, gathered):
        partial_value = lax.dot_general(
            cotangent, acts, (((0,), (0,)), ((), ())), preferred_element_type=jnp.float32
        ).astype(jnp.bfloat16)
        gradient = lax.psum_scatter(partial_value, "y", scatter_dimension=0, tiled=True)
        master_new, update = adamw(
            gradient.astype(jnp.float32),
            master[:, low:high],
            first_moment[:, low:high].astype(jnp.float32),
            second_moment[:, low:high].astype(jnp.float32),
            first_fix,
            second_fix,
        )
        updates[low] = update
        weights[low] = master_new.astype(jnp.bfloat16)
    order = sorted(updates)
    head = weights[order[0]][:, :DRIFT]
    tail = weights[order[-1]][:, -DRIFT:]
    ends = tensor_count - 1
    left = lax.ppermute(tail, TENSOR, [(i, i + 1) for i in range(ends)])
    right = lax.ppermute(head, TENSOR, [(i + 1, i) for i in range(ends)])
    position = lax.axis_index(TENSOR)
    places = jnp.arange(tensor_count, dtype=jnp.int32)
    first_slot = jnp.sum(jnp.where(places < position, row_counts, 0))
    length = jnp.sum(jnp.where(places == position, row_counts, 0))
    rows = master.shape[0]
    widened = jnp.concatenate(
        [left] + [weights[k] for k in order] + [right, jnp.zeros((rows, 2 * DRIFT), jnp.bfloat16)],
        axis=1,
    )
    start = first_slot - position * width + DRIFT
    window = lax.dynamic_slice_in_dim(widened, start, CAP, 1)
    slot_index = jnp.arange(CAP, dtype=jnp.int32)
    laid = jnp.where((slot_index < length)[None, :], window, jnp.zeros((), jnp.bfloat16))
    return (jnp.concatenate([updates[k] for k in order], axis=1), laid)


def solution(mesh):
    fine = Mesh(np.asarray(mesh.devices).reshape(8, 4, 4, 2), ("z", "y", "x", "core"))
    dp = ("z", "y")
    return jax.shard_map(
        per_device,
        mesh=fine,
        in_specs=(
            P(dp, TENSOR),
            P(dp + TENSOR, None),
            P(dp, TENSOR),
            P(dp, TENSOR),
            P(dp, TENSOR),
            P(),
            P(),
        ),
        out_specs=(P(dp, TENSOR), P(dp, TENSOR)),
        check_vma=False,
    )
```

profile of v0, /device:TPU:2, one launch (start us, length us, event | category | flops | bytes accessed | tf_op | source)
XLA Modules:
  0.0 358.5 jit_solution(4531047940108893145)
XLA Ops:
  8.2 20.2 %all_to_all.19 = bf16[16,8,1024]{2,0,1:T(8,128)(2,1)} all-to-all(bf16[16,8,1024]{2,0,1:T(8,128)(2,1)S(1)} %bitcast.27), channel_id=1, replica_groups=mesh['z'=8,'y'=4,'x'=4,'core'=2] {'z'}, dimensions={1} | all-to-all | bytes 524288 | tf_op jit(solution)/shard_map/all_to_all | solution.py:34
  28.5 1.9 fusion.41
  33.6 18.1 %all-gather.6.cloned.1.call-done = bf16[1024,1024]{1,0:T(8,128)(2,1)} async-done(((bf16[128,1024]{1,0:T(8,128)(2,1)}), bf16[1024,1024]{1,0:T(8,128)(2,1)}) %all-gather.6.cloned.1.call-update) | async-done | bytes 2097168 | tf_op jit(solution)/shard_map/all_gather | solution.py:35
  53.5 42.4 %all-gather.14.cloned.1.call-done = bf16[1024,896]{1,0:T(8,128)(2,1)} async-done(((bf16[128,896]{1,0:T(8,128)(2,1)}), bf16[1024,896]{1,0:T(8,128)(2,1)}) %all-gather.14.cloned.1.call-update) | async-done | bytes 1835024 | tf_op jit(solution)/shard_map/all_gather | solution.py:42
  95.9 5.1 %convolution_convert_fusion = bf16[1024,896]{1,0:T(8,128)(2,1)} fusion(bf16[1024,1024]{1,0:T(8,128)(2,1)S(1)} %bitcast.22, bf16[1024,896]{1,0:T(8,128)(2,1)} %all-gather.14.cloned.1.call-done), kind=kOutput, calls=%fused_computation.2 | convolution fusion | flops 1879965696 | bytes 5767168 | tf_op jit(solution)/shard_map/dot_general | solution.py:47
  101.1 36.4 %all-gather.8.cloned.1.call-done = bf16[1024,896]{1,0:T(8,128)(2,1)} async-done(((bf16[128,896]{1,0:T(8,128)(2,1)}), bf16[1024,896]{1,0:T(8,128)(2,1)}) %all-gather.8.cloned.1.call-update) | async-done | bytes 1835024 | tf_op jit(solution)/shard_map/all_gather | solution.py:42
  137.5 5.1 %convolution_convert_fusion.1 = bf16[1024,896]{1,0:T(8,128)(2,1)} fusion(bf16[1024,1024]{1,0:T(8,128)(2,1)S(1)} %bitcast.23, bf16[1024,896]{1,0:T(8,128)(2,1)} %all-gather.8.cloned.1.call-done), kind=kOutput, calls=%fused_computation.3 | convolution fusion | flops 1879965696 | bytes 5767168 | tf_op jit(solution)/shard_map/dot_general | solution.py:47
  142.7 35.1 %all-gather.10.cloned.1.call-done = bf16[1024,768]{1,0:T(8,128)(2,1)} async-done(((bf16[128,768]{1,0:T(8,128)(2,1)}), bf16[1024,768]{1,0:T(8,128)(2,1)}) %all-gather.10.cloned.1.call-update) | async-done | bytes 1572880 | tf_op jit(solution)/shard_map/all_gather | solution.py:42
  177.7 4.4 %convolution_convert_fusion.3 = bf16[1024,768]{1,0:T(8,128)(2,1)} fusion(bf16[1024,1024]{1,0:T(8,128)(2,1)S(1)} %bitcast.24, bf16[1024,768]{1,0:T(8,128)(2,1)} %all-gather.10.cloned.1.call-done), kind=kOutput, calls=%fused_computation.5 | convolution fusion | flops 1611399168 | bytes 5242880 | tf_op jit(solution)/shard_map/dot_general | solution.py:47
  182.2 35.8 %all-gather.12.cloned.1.call-done = bf16[1024,768]{1,0:T(8,128)(2,1)} async-done(((bf16[128,768]{1,0:T(8,128)(2,1)}), bf16[1024,768]{1,0:T(8,128)(2,1)}) %all-gather.12.cloned.1.call-update) | async-done | bytes 1572880 | tf_op jit(solution)/shard_map/all_gather | solution.py:42
  218.0 4.4 %convolution_convert_fusion.2 = bf16[1024,768]{1,0:T(8,128)(2,1)} fusion(bf16[1024,1024]{1,0:T(8,128)(2,1)S(1)} %bitcast.25, bf16[1024,768]{1,0:T(8,128)(2,1)} %all-gather.12.cloned.1.call-done), kind=kOutput, calls=%fused_computation.4 | convolution fusion | flops 1611399168 | bytes 5242880 | tf_op jit(solution)/shard_map/dot_general | solution.py:47
  223.2 26.5 %reduce-scatter.11.cloned.1.call-done = bf16[256,896]{1,0:T(8,128)(2,1)} async-done(((bf16[1024,896]{1,0:T(8,128)(2,1)}), bf16[256,896]{1,0:T(8,128)(2,1)}) %reduce-scatter.11.cloned.1.call-update) | async-done | bytes 458768 | tf_op jit(solution)/shard_map/reduce_scatter | solution.py:50
  249.8 2.4 subtract_convert_fusion.1
  252.1 1.9 collective-permute-start
  256.0 2.5 collective-permute-done
  259.1 23.7 %reduce-scatter.5.cloned.1.call-done = bf16[256,896]{1,0:T(8,128)(2,1)} async-done(((bf16[1024,896]{1,0:T(8,128)(2,1)}), bf16[256,896]{1,0:T(8,128)(2,1)}) %reduce-scatter.5.cloned.1.call-update) | async-done | bytes 458768 | tf_op jit(solution)/shard_map/reduce_scatter | solution.py:50
  282.8 3.2 constant_dynamic-update-slice_fusion.2
  286.0 2.1 collective-permute-start.1
  288.2 25.2 %reduce-scatter.7.cloned.1.call-done = bf16[256,768]{1,0:T(8,128)(2,1)} async-done(((bf16[1024,768]{1,0:T(8,128)(2,1)}), bf16[256,768]{1,0:T(8,128)(2,1)}) %reduce-scatter.7.cloned.1.call-update) | async-done | bytes 393232 | tf_op jit(solution)/shard_map/reduce_scatter | solution.py:50
  313.3 3.0 fusion.32
  316.3 27.6 %reduce-scatter.9.cloned.1.call-done = bf16[256,768]{1,0:T(8,128)(2,1)} async-done(((bf16[1024,768]{1,0:T(8,128)(2,1)}), bf16[256,768]{1,0:T(8,128)(2,1)}) %reduce-scatter.9.cloned.1.call-update) | async-done | bytes 393232 | tf_op jit(solution)/shard_map/reduce_scatter | solution.py:50
  343.9 2.9 fusion.33
  346.9 2.0 pad_maximum_fusion
  349.7 2.4 dynamic-slice_select_fusion
  (34 shorter events, 9.0 us)
Async XLA Ops:
  7.2 44.6 %all-gather.6.cloned.1.call-start = ((), (), s32[]{:S(2)}) async-start(), calls=%async_computation.5 | async-start | bytes 2359296 | tf_op jit(solution)/shard_map/all_gather | solution.py:35
  28.5 67.5 %all-gather.14.cloned.1.call-start = ((), (), s32[]{:S(2)}) async-start(), calls=%async_computation.12 | async-start | bytes 2064384 | tf_op jit(solution)/shard_map/all_gather | solution.py:42
  30.4 107.1 %all-gather.8.cloned.1.call-start = ((), (), s32[]{:S(2)}) async-start(), calls=%async_computation.6 | async-start | bytes 2064384 | tf_op jit(solution)/shard_map/all_gather | solution.py:42
  31.1 146.6 %all-gather.10.cloned.1.call-start = ((), (), s32[]{:S(2)}) async-start(), calls=%async_computation.8 | async-start | bytes 1769472 | tf_op jit(solution)/shard_map/all_gather | solution.py:42
  33.0 185.0 %all-gather.12.cloned.1.call-start = ((), (), s32[]{:S(2)}) async-start(), calls=%async_computation.10 | async-start | bytes 1769472 | tf_op jit(solution)/shard_map/all_gather | solution.py:42
  33.6 216.2 %reduce-scatter.11.cloned.1.call-start = ((), (), s32[]{:S(2)}) async-start(), calls=%async_computation.13 | async-start | bytes 2293760 | tf_op jit(solution)/shard_map/reduce_scatter | solution.py:50
  101.1 181.7 %reduce-scatter.5.cloned.1.call-start = ((), (), s32[]{:S(2)}) async-start(), calls=%async_computation.7 | async-start | bytes 2293760 | tf_op jit(solution)/shard_map/reduce_scatter | solution.py:50
  142.6 170.7 %reduce-scatter.7.cloned.1.call-start = ((), (), s32[]{:S(2)}) async-start(), calls=%async_computation.9 | async-start | bytes 1966080 | tf_op jit(solution)/shard_map/reduce_scatter | solution.py:50
  182.2 161.8 %reduce-scatter.9.cloned.1.call-start = ((), (), s32[]{:S(2)}) async-start(), calls=%async_computation.11 | async-start | bytes 1966080 | tf_op jit(solution)/shard_map/reduce_scatter | solution.py:50
  222.5 31.6 %copy-start.1 = (s32[8]{0:T(128)S(1)}, s32[8]{0:T(128)}, u32[]{:S(2)}) copy-start(s32[8]{0:T(128)} %param.12) | copy-start | bytes 100
  252.1 6.3 %collective-permute-start = (bf16[256,256]{1,0:T(8,128)(2,1)S(1)}, bf16[256,256]{1,0:T(8,128)(2,1)S(1)}, u32[]{:S(2)}, u32[]{:S(2)}) collective-permute-start(bf16[256,256]{1,0:T(8,128)(2,1)S(1)} %slice.72), channel_id=1, source_target_pairs={{0,1},{1,2},{2,3},{3,4},{4,5},{5,6},{6,7},{8,9},{9,10},{10,11},{11... | collective-permute-start | bytes 393224 | tf_op jit(solution)/shard_map/ppermute | solution.py:65
  286.0 63.6 %collective-permute-start.1 = (bf16[256,256]{1,0:T(8,128)(2,1)S(1)}, bf16[256,256]{1,0:T(8,128)(2,1)S(1)}, u32[]{:S(2)}, u32[]{:S(2)}) collective-permute-start(bf16[256,256]{1,0:T(8,128)(2,1)S(1)} %slice.73), channel_id=1, source_target_pairs={{1,0},{2,1},{3,2},{4,3},{5,4},{6,5},{7,6},{9,8},{10,9},{11,10},{12... | collective-permute-start | bytes 393224 | tf_op jit(solution)/shard_map/ppermute | solution.py:66
  346.9 2.7 copy-start
Sparse Core Ops, SparseCore 0:
  28.6 23.1 all-gather.5
  54.1 41.7 all-gather.13
  98.3 39.1 all-gather.7
  139.1 38.5 all-gather.9
  179.4 38.5 all-gather.11
  221.0 28.7 reduce-scatter.10
  252.9 29.8 reduce-scatter.4
  285.3 27.9 reduce-scatter.6
  315.9 27.9 reduce-scatter.8
where the time goes:
time: 359 us
  waiting for transfers between devices  275 us (77%)
  blocking collectives  20.2 us (6%)
  matrix products  19.1 us (5%)
  other arithmetic  17.1 us (5%)
  between operations  15.3 us (4%)
  local copies, waits for them, and re-layouts  7.9 us (2%)
  starting transfers between devices  4.42 us (1%)
    all_gather x4, waiting for transfers between devices, per_device(): lax.all_gather(hidden[:, low:high], 'z', axis=0, tiled=True)  150 us
    reduce_scatter x4, waiting for transfers between devices, per_device(): lax.psum_scatter(partial_value, 'y', scatter_dimension=0, tiled=True)  103 us
    all_to_all x1, blocking collectives, per_device(): lax.all_to_all(out_grad, 'z', split_axis=1, concat_axis=0, tiled=True)  20.2 us
    dot_general x4, matrix products, per_device(): lax.dot_general(cotangent, acts, (((0,), (0,)), ((), ())), preferred_elem...  19.1 us
    all_gather x1, waiting for transfers between devices, per_device(): spread = lax.all_gather(regrouped, TENSOR, axis=0, tiled=True)  18.1 us
    unnamed x3, other arithmetic  9.14 us
  transfers between devices with their start and end apart: 11, of which 10 were waited for; matrix products, arithmetic and copies ran while one was open for 11% of the time, Pallas kernels for 0%

commit v1 on v0

--- a/solution.py
+++ b/solution.py
@@ -31,7 +31,10 @@
     z_count = lax.axis_size("z")
     local_tokens = out_grad.shape[0]
     features = out_grad.shape[1] // z_count
-    regrouped = lax.all_to_all(out_grad, "z", split_axis=1, concat_axis=0, tiled=True)
+    size = lax.axis_size("z")
+    parts = jnp.stack(jnp.split(out_grad, size, axis=1), axis=0)
+    parts = lax.all_to_all(parts, "z", split_axis=0, concat_axis=0)
+    regrouped = jnp.concatenate(parts, axis=0)
     spread = lax.all_gather(regrouped, TENSOR, axis=0, tiled=True)
     cotangent = spread.reshape(tensor_count, z_count, local_tokens, features)
     cotangent = cotangent.transpose(1, 0, 2, 3).reshape(-1, features)

time: 359 us -> 365 us (1.017)
  local copies, waits for them, and re-layouts: 7.9 us -> 13 us
    unnamed x7 -> x14, local copies, waits for them, and re-layouts: 1.46 us -> 6.78 us
where the time goes in v1:
time: 365 us; the launch traced here: 364 us
  waiting for transfers between devices  275 us (75%)
  blocking collectives  20.2 us (6%)
  matrix products  19.1 us (5%)
  other arithmetic  17.1 us (5%)
  between operations  15.3 us (4%)
  local copies, waits for them, and re-layouts  13 us (4%)
  starting transfers between devices  4.42 us (1%)
    all_gather x4, waiting for transfers between devices, per_device(): lax.all_gather(hidden[:, low:high], 'z', axis=0, tiled=True)  150 us
    reduce_scatter x4, waiting for transfers between devices, per_device(): lax.psum_scatter(partial_value, 'y', scatter_dimension=0, tiled=True)  103 us
    all_to_all x1, blocking collectives, per_device(): parts = lax.all_to_all(parts, 'z', split_axis=0, concat_axis=0)  20.2 us
    dot_general x4, matrix products, per_device(): lax.dot_general(cotangent, acts, (((0,), (0,)), ((), ())), preferred_elem...  19.1 us
    all_gather x1, waiting for transfers between devices, per_device(): spread = lax.all_gather(regrouped, TENSOR, axis=0, tiled=True)  18.1 us
    unnamed x3, other arithmetic  9.14 us
  transfers between devices with their start and end apart: 11, of which 10 were waited for; matrix products, arithmetic and copies ran while one was open for 11% of the time, Pallas kernels for 0%

profile of v1, /device:TPU:2, one launch (start us, length us, event | category | flops | bytes accessed | tf_op | source)
XLA Modules:
  0.0 363.6 jit_solution(16588130567693831979)
XLA Ops:
  13.3 20.2 %all_to_all.5 = bf16[8,16,1024]{2,1,0:T(8,128)(2,1)} all-to-all(bf16[8,16,1024]{2,1,0:T(8,128)(2,1)S(1)} %constant_dynamic-update-slice_fusion), channel_id=1, replica_groups=mesh['z'=8,'y'=4,'x'=4,'core'=2] {'z'}, dimensions={0} | all-to-all | bytes 524288 | tf_op jit(solution)/shard_map/all_to_all | solution.py:36
  33.6 1.9 fusion.41
  38.7 18.1 %all-gather.6.cloned.1.call-done = bf16[1024,1024]{1,0:T(8,128)(2,1)} async-done(((bf16[128,1024]{1,0:T(8,128)(2,1)}), bf16[1024,1024]{1,0:T(8,128)(2,1)}) %all-gather.6.cloned.1.call-update) | async-done | bytes 2097168 | tf_op jit(solution)/shard_map/all_gather | solution.py:38
  58.6 42.4 %all-gather.14.cloned.1.call-done = bf16[1024,896]{1,0:T(8,128)(2,1)} async-done(((bf16[128,896]{1,0:T(8,128)(2,1)}), bf16[1024,896]{1,0:T(8,128)(2,1)}) %all-gather.14.cloned.1.call-update) | async-done | bytes 1835024 | tf_op jit(solution)/shard_map/all_gather | solution.py:45
  101.0 5.1 %convolution_convert_fusion = bf16[1024,896]{1,0:T(8,128)(2,1)} fusion(bf16[1024,1024]{1,0:T(8,128)(2,1)S(1)} %bitcast.32, bf16[1024,896]{1,0:T(8,128)(2,1)} %all-gather.14.cloned.1.call-done), kind=kOutput, calls=%fused_computation.2 | convolution fusion | flops 1879965696 | bytes 5767168 | tf_op jit(solution)/shard_map/dot_general | solution.py:50
  106.2 36.4 %all-gather.8.cloned.1.call-done = bf16[1024,896]{1,0:T(8,128)(2,1)} async-done(((bf16[128,896]{1,0:T(8,128)(2,1)}), bf16[1024,896]{1,0:T(8,128)(2,1)}) %all-gather.8.cloned.1.call-update) | async-done | bytes 1835024 | tf_op jit(solution)/shard_map/all_gather | solution.py:45
  142.6 5.1 %convolution_convert_fusion.1 = bf16[1024,896]{1,0:T(8,128)(2,1)} fusion(bf16[1024,1024]{1,0:T(8,128)(2,1)S(1)} %bitcast.33, bf16[1024,896]{1,0:T(8,128)(2,1)} %all-gather.8.cloned.1.call-done), kind=kOutput, calls=%fused_computation.3 | convolution fusion | flops 1879965696 | bytes 5767168 | tf_op jit(solution)/shard_map/dot_general | solution.py:50
  147.8 35.1 %all-gather.10.cloned.1.call-done = bf16[1024,768]{1,0:T(8,128)(2,1)} async-done(((bf16[128,768]{1,0:T(8,128)(2,1)}), bf16[1024,768]{1,0:T(8,128)(2,1)}) %all-gather.10.cloned.1.call-update) | async-done | bytes 1572880 | tf_op jit(solution)/shard_map/all_gather | solution.py:45
  182.8 4.4 %convolution_convert_fusion.3 = bf16[1024,768]{1,0:T(8,128)(2,1)} fusion(bf16[1024,1024]{1,0:T(8,128)(2,1)S(1)} %bitcast.34, bf16[1024,768]{1,0:T(8,128)(2,1)} %all-gather.10.cloned.1.call-done), kind=kOutput, calls=%fused_computation.5 | convolution fusion | flops 1611399168 | bytes 5242880 | tf_op jit(solution)/shard_map/dot_general | solution.py:50
  187.3 35.8 %all-gather.12.cloned.1.call-done = bf16[1024,768]{1,0:T(8,128)(2,1)} async-done(((bf16[128,768]{1,0:T(8,128)(2,1)}), bf16[1024,768]{1,0:T(8,128)(2,1)}) %all-gather.12.cloned.1.call-update) | async-done | bytes 1572880 | tf_op jit(solution)/shard_map/all_gather | solution.py:45
  223.1 4.4 %convolution_convert_fusion.2 = bf16[1024,768]{1,0:T(8,128)(2,1)} fusion(bf16[1024,1024]{1,0:T(8,128)(2,1)S(1)} %bitcast.35, bf16[1024,768]{1,0:T(8,128)(2,1)} %all-gather.12.cloned.1.call-done), kind=kOutput, calls=%fused_computation.4 | convolution fusion | flops 1611399168 | bytes 5242880 | tf_op jit(solution)/shard_map/dot_general | solution.py:50
  228.3 26.5 %reduce-scatter.11.cloned.1.call-done = bf16[256,896]{1,0:T(8,128)(2,1)} async-done(((bf16[1024,896]{1,0:T(8,128)(2,1)}), bf16[256,896]{1,0:T(8,128)(2,1)}) %reduce-scatter.11.cloned.1.call-update) | async-done | bytes 458768 | tf_op jit(solution)/shard_map/reduce_scatter | solution.py:53
  254.9 2.4 subtract_convert_fusion.1
  257.3 1.9 collective-permute-start
  261.1 2.5 collective-permute-done
  264.2 23.7 %reduce-scatter.5.cloned.1.call-done = bf16[256,896]{1,0:T(8,128)(2,1)} async-done(((bf16[1024,896]{1,0:T(8,128)(2,1)}), bf16[256,896]{1,0:T(8,128)(2,1)}) %reduce-scatter.5.cloned.1.call-update) | async-done | bytes 458768 | tf_op jit(solution)/shard_map/reduce_scatter | solution.py:53
  287.9 3.2 constant_dynamic-update-slice_fusion.10
  291.1 2.1 collective-permute-start.1
  293.3 25.2 %reduce-scatter.7.cloned.1.call-done = bf16[256,768]{1,0:T(8,128)(2,1)} async-done(((bf16[1024,768]{1,0:T(8,128)(2,1)}), bf16[256,768]{1,0:T(8,128)(2,1)}) %reduce-scatter.7.cloned.1.call-update) | async-done | bytes 393232 | tf_op jit(solution)/shard_map/reduce_scatter | solution.py:53
  318.4 3.0 fusion.32
  321.4 27.6 %reduce-scatter.9.cloned.1.call-done = bf16[256,768]{1,0:T(8,128)(2,1)} async-done(((bf16[1024,768]{1,0:T(8,128)(2,1)}), bf16[256,768]{1,0:T(8,128)(2,1)}) %reduce-scatter.9.cloned.1.call-update) | async-done | bytes 393232 | tf_op jit(solution)/shard_map/reduce_scatter | solution.py:53
  349.0 2.9 fusion.33
  352.0 2.0 pad_maximum_fusion
  354.8 2.4 dynamic-slice_select_fusion
  (41 shorter events, 14.1 us)
Async XLA Ops:
  7.2 49.7 %all-gather.6.cloned.1.call-start = ((), (), s32[]{:S(2)}) async-start(), calls=%async_computation.5 | async-start | bytes 2359296 | tf_op jit(solution)/shard_map/all_gather | solution.py:38
  33.6 67.5 %all-gather.14.cloned.1.call-start = ((), (), s32[]{:S(2)}) async-start(), calls=%async_computation.12 | async-start | bytes 2064384 | tf_op jit(solution)/shard_map/all_gather | solution.py:45
  35.5 107.1 %all-gather.8.cloned.1.call-start = ((), (), s32[]{:S(2)}) async-start(), calls=%async_computation.6 | async-start | bytes 2064384 | tf_op jit(solution)/shard_map/all_gather | solution.py:45
  36.2 146.6 %all-gather.10.cloned.1.call-start = ((), (), s32[]{:S(2)}) async-start(), calls=%async_computation.8 | async-start | bytes 1769472 | tf_op jit(solution)/shard_map/all_gather | solution.py:45
  38.1 185.0 %all-gather.12.cloned.1.call-start = ((), (), s32[]{:S(2)}) async-start(), calls=%async_computation.10 | async-start | bytes 1769472 | tf_op jit(solution)/shard_map/all_gather | solution.py:45
  38.7 216.2 %reduce-scatter.11.cloned.1.call-start = ((), (), s32[]{:S(2)}) async-start(), calls=%async_computation.13 | async-start | bytes 2293760 | tf_op jit(solution)/shard_map/reduce_scatter | solution.py:53
  106.2 181.7 %reduce-scatter.5.cloned.1.call-start = ((), (), s32[]{:S(2)}) async-start(), calls=%async_computation.7 | async-start | bytes 2293760 | tf_op jit(solution)/shard_map/reduce_scatter | solution.py:53
  147.7 170.7 %reduce-scatter.7.cloned.1.call-start = ((), (), s32[]{:S(2)}) async-start(), calls=%async_computation.9 | async-start | bytes 1966080 | tf_op jit(solution)/shard_map/reduce_scatter | solution.py:53
  187.3 161.7 %reduce-scatter.9.cloned.1.call-start = ((), (), s32[]{:S(2)}) async-start(), calls=%async_computation.11 | async-start | bytes 1966080 | tf_op jit(solution)/shard_map/reduce_scatter | solution.py:53
  227.6 31.6 %copy-start.1 = (s32[8]{0:T(128)S(1)}, s32[8]{0:T(128)}, u32[]{:S(2)}) copy-start(s32[8]{0:T(128)} %param.12) | copy-start | bytes 100
  257.3 6.3 %collective-permute-start = (bf16[256,256]{1,0:T(8,128)(2,1)S(1)}, bf16[256,256]{1,0:T(8,128)(2,1)S(1)}, u32[]{:S(2)}, u32[]{:S(2)}) collective-permute-start(bf16[256,256]{1,0:T(8,128)(2,1)S(1)} %slice.72), channel_id=1, source_target_pairs={{0,1},{1,2},{2,3},{3,4},{4,5},{5,6},{6,7},{8,9},{9,10},{10,11},{11... | collective-permute-start | bytes 393224 | tf_op jit(solution)/shard_map/ppermute | solution.py:68
  291.1 63.6 %collective-permute-start.1 = (bf16[256,256]{1,0:T(8,128)(2,1)S(1)}, bf16[256,256]{1,0:T(8,128)(2,1)S(1)}, u32[]{:S(2)}, u32[]{:S(2)}) collective-permute-start(bf16[256,256]{1,0:T(8,128)(2,1)S(1)} %slice.73), channel_id=1, source_target_pairs={{1,0},{2,1},{3,2},{4,3},{5,4},{6,5},{7,6},{9,8},{10,9},{11,10},{12... | collective-permute-start | bytes 393224 | tf_op jit(solution)/shard_map/ppermute | solution.py:69
  352.0 2.7 copy-start
Sparse Core Ops, SparseCore 0:
  33.7 23.1 all-gather.5
  59.2 41.7 all-gather.13
  103.4 39.1 all-gather.7
  144.2 38.5 all-gather.9
  184.5 38.5 all-gather.11
  226.1 28.7 reduce-scatter.10
  258.0 29.8 reduce-scatter.4
  290.4 27.9 reduce-scatter.6
  321.0 27.9 reduce-scatter.8
